TPU v7x, 32 devices: a whole 2x2x4 slice. The times are simulated.
32 devices in a mesh: re: 8 (over y, x, core), rp: 4 (over z).
Axes of the slice: x: 2, y: 2, z: 4, core: 2. Of those that a mesh axis runs over, the one named last changes fastest.
Arguments:
- wannier_table: bfloat16 [1024, 128, 1536], P('re', 'rp'), may hold values from -0.0078125 to 0.0078125
- mode_matrix: float32 [2, 12, 12], replicated, may hold values from -1.75 to 1.75
- re_coords: int32 [3, 1024], replicated, may hold values from -8 to 8
- rp_coords: int32 [3, 128], P(None, 'rp'), may hold values from -6 to 6
- q_coords: int32 [3, 2], replicated, may hold values from 0 to 63
- k_coords: int32 [3, 4096], P(None, 're'), may hold values from 0 to 63
- rotations: bfloat16 [4096, 128], P('re'), may hold values from -1.5 to 1.5
- kq_owner: int32 [2, 4096, 1], P(None, 're'), may hold values from 0 to 7; in each aligned block of 512 rows (0 to 511, 512 to 1023, ..., all dimensions but the last counted through in order) at most 96 rows name the same one
- kq_row: int32 [2, 4096], P(None, 're'), may hold values from 0 to 511
Outputs:
- couplings: bfloat16 [2, 12, 2, 64, 4096], P(None, 'rp', None, None, 're')
Inputs may be any that keep to these rules, and one draw needn't show every extreme that they name: `kq_owner`: for each wavevector, among the 512 k-rows of one device no owner is named more than 96 times, a bound that some block reaches.
All inputs are finite; a program needn't handle non-finite values.
Results may differ from a plain program's by a relative error of at most 0.0057.
Values may be sent and summed in bfloat16 or wider, within the bound.
A program may use at most 128 MiB of HBM per device.

v0:
```python
import functools
import math

import jax
import jax.numpy as jnp
from jax import lax
from jax.experimental import pallas as pl
from jax.experimental.pallas import tpu as pltpu
from jax.sharding import PartitionSpec as P

NB = 8
MODES = 12
Q = 2
GRID = 64
GROUP = 8
F32 = jnp.float32
BF16 = jnp.bfloat16


def phases(left, right):
    products = jnp.sum(left[:, :, None] * right[:, None, :], axis=0)
    angles = jnp.mod(products, GRID).astype(F32) * (2.0 * math.pi / GRID)
    return (jnp.cos(angles).astype(BF16), jnp.sin(angles).astype(BF16))


def sine_turn(turn):
    x = turn * (2.0 * math.pi)
    y = x * x
    p = 2.75573192e-6 - y * 2.50521084e-8
    p = -1.98412698e-4 + y * p
    p = 8.33333333e-3 + y * p
    p = -1.66666667e-1 + y * p
    return x + x * (y * p)


def mix_kernel(phase_ref, modes_ref, table_ref, out_ref, summed, kron):
    step = pl.program_id(0)
    block, r_local, both = table_ref.shape
    width = both // 2
    e_local = summed.shape[1] // 2
    owners, _, depth, _ = out_ref.shape

    @pl.when(step == 0)
    def _():
        shape = (MODES, width)
        expand = (
            lax.broadcasted_iota(jnp.int32, shape, 1) // (NB * NB)
            == lax.broadcasted_iota(jnp.int32, shape, 0)
        ).astype(F32).astype(BF16)
        rows = lax.broadcasted_iota(jnp.int32, (width, width), 0) & (NB * NB - 1)
        cols = lax.broadcasted_iota(jnp.int32, (width, width), 1) & (NB * NB - 1)
        for q in range(Q):
            spread = jnp.dot(modes_ref[q], expand, preferred_element_type=F32)
            kron[q] = jnp.where(rows == cols, spread, 0.0).astype(BF16)

    parts = []
    for g in range(block // GROUP):
        values = table_ref[g * GROUP : (g + 1) * GROUP].reshape(GROUP * r_local, both)
        parts.append(
            jnp.dot(phase_ref[0], values[:, :width], preferred_element_type=F32)
            + jnp.dot(phase_ref[1], values[:, width:], preferred_element_type=F32)
        )
    for q in range(Q):
        for c in range(2):
            first = (q * 2 + c) * GROUP
            rows = jnp.concatenate([part[first : first + GROUP] for part in parts], axis=0)
            start = pl.multiple_of(c * e_local + step * block, block)
            summed[q, pl.ds(start, block), :] = rows.astype(BF16)

    @pl.when(step == pl.num_programs(0) - 1)
    def _():
        for q in range(Q):
            mixed = lax.dot_general(
                kron[q], summed[q], (((1,), (1,)), ((), ())), preferred_element_type=F32
            ).astype(out_ref.dtype)
            for owner in range(owners):
                out_ref[owner, q] = mixed[owner * depth : (owner + 1) * depth]


def mix(phase, modes, table, owners):
    e_local, r_local, both = table.shape
    width = both // 2
    block = 16
    out_shape = (owners, Q, width // owners, 2 * e_local)
    return pl.pallas_call(
        mix_kernel,
        grid=(e_local // block,),
        in_specs=[
            pl.BlockSpec(phase.shape, lambda i: (0, 0, 0)),
            pl.BlockSpec(modes.shape, lambda i: (0, 0, 0)),
            pl.BlockSpec((block, r_local, both), lambda i: (i, 0, 0)),
        ],
        out_specs=pl.BlockSpec(out_shape, lambda i: (0, 0, 0, 0)),
        out_shape=jax.ShapeDtypeStruct(out_shape, BF16),
        scratch_shapes=[
            pltpu.VMEM((Q, 2 * e_local, width), BF16),
            pltpu.VMEM((Q, width, width), BF16),
        ],
        compiler_params=pltpu.CompilerParams(vmem_limit_bytes=40 << 20),
    )(phase, modes, table)


def bloch_kernel(
    coupling_ref, re_ref, k_ref, near_ref, all_ref, owner_ref, row_ref, out_ref,
    cosine, sine, summed, near, far,
):
    devices, _, depth, twice = coupling_ref.shape
    e_local = twice // 2
    k_local = k_ref.shape[1]
    modes_local = depth // (NB * NB)
    pairs = NB * NB
    near[...] = near_ref[...].astype(F32)

    @pl.loop(0, Q)
    def _(q):
        rows = lax.broadcasted_iota(jnp.int32, (k_local, k_local), 0)
        hot = (rows == row_ref[q]).astype(F32).astype(BF16)
        owner = owner_ref[q]
        far[q] = jnp.zeros(far.shape[1:], F32)

        @pl.loop(0, devices)
        def _(d):
            found = jnp.dot(all_ref[d], hot, preferred_element_type=F32)
            far[q] = jnp.where(owner == d, found, far[q])

    @pl.loop(0, devices)
    def _(d):
        start = pl.multiple_of(d * e_local, e_local)
        turns = jnp.dot(
            re_ref[pl.ds(start, e_local), :], k_ref[...], preferred_element_type=F32
        ) * (1.0 / GRID)
        turns = turns - jnp.floor(turns + 0.5)
        cosine[pl.ds(start, e_local), :] = sine_turn(0.25 - jnp.abs(turns)).astype(BF16)
        folded = jnp.maximum(jnp.minimum(turns, 0.5 - turns), -0.5 - turns)
        sine[pl.ds(start, e_local), :] = sine_turn(folded).astype(BF16)

    tile = min(256, k_local)

    @pl.loop(0, Q)
    def _(q):
        left = jnp.concatenate(
            [
                jnp.concatenate([coupling_ref[d, q, :, :e_local] for d in range(devices)], axis=1),
                jnp.concatenate([coupling_ref[d, q, :, e_local:] for d in range(devices)], axis=1),
            ],
            axis=0,
        )

        @pl.loop(0, k_local // tile)
        def _(j):
            cols = pl.ds(pl.multiple_of(j * tile, tile), tile)
            with_cos = jnp.dot(left, cosine[:, cols], preferred_element_type=F32)
            with_sin = jnp.dot(left, sine[:, cols], preferred_element_type=F32)
            real = with_cos[:depth] - with_sin[depth:]
            imag = with_cos[depth:] + with_sin[:depth]
            for v in range(modes_local):
                summed[q, 0, v, :, cols] = real[v * pairs : (v + 1) * pairs]
                summed[q, 1, v, :, cols] = imag[v * pairs : (v + 1) * pairs]

    lanes = 128
    tiles = k_local // lanes

    @pl.loop(0, Q * modes_local * tiles)
    def _(i):
        q = i // (modes_local * tiles)
        v = (i // tiles) % modes_local
        cols = pl.ds(pl.multiple_of((i % tiles) * lanes, lanes), lanes)

        def spread(ref, lead, row):
            return jnp.broadcast_to(ref[lead + (pl.ds(row, 1), cols)], (NB, lanes))

        right_real = [near[pl.ds(b * NB, NB), cols] for b in range(NB)]
        right_imag = [near[pl.ds(pairs + b * NB, NB), cols] for b in range(NB)]
        half_real, half_imag = [], []
        for a in range(NB):
            real = imag = None
            for b in range(NB):
                c_real = spread(summed, (q, 0, v), a * NB + b)
                c_imag = spread(summed, (q, 1, v), a * NB + b)
                one = c_real * right_real[b] - c_imag * right_imag[b]
                two = c_real * right_imag[b] + c_imag * right_real[b]
                real = one if real is None else real + one
                imag = two if imag is None else imag + two
            half_real.append(real)
            half_imag.append(imag)
        for m in range(0, NB, 2):
            reals, imags = [], []
            for n in (m, m + 1):
                real = imag = None
                for a in range(NB):
                    l_real = spread(far, (q,), a * NB + n)
                    l_imag = spread(far, (q,), pairs + a * NB + n)
                    one = l_real * half_real[a] + l_imag * half_imag[a]
                    two = l_real * half_imag[a] - l_imag * half_real[a]
                    real = one if real is None else real + one
                    imag = two if imag is None else imag + two
                reals.append(real)
                imags.append(imag)
            rows = pl.ds(m * NB, 2 * NB)
            out_ref[q, v, 0, rows, cols] = jnp.concatenate(reals, axis=0).astype(BF16)
            out_ref[q, v, 1, rows, cols] = jnp.concatenate(imags, axis=0).astype(BF16)


def bloch(coupling, re_rows, k_cols, near, everyone, owner, row):
    devices, _, depth, _ = coupling.shape
    e_all = re_rows.shape[0]
    k_local = k_cols.shape[1]
    modes_local = depth // (NB * NB)
    return pl.pallas_call(
        bloch_kernel,
        in_specs=[pl.BlockSpec(memory_space=pltpu.VMEM)] * 7,
        out_specs=pl.BlockSpec(memory_space=pltpu.VMEM),
        out_shape=jax.ShapeDtypeStruct((Q, modes_local, 2, NB * NB, k_local), BF16),
        scratch_shapes=[
            pltpu.VMEM((e_all, k_local), BF16),
            pltpu.VMEM((e_all, k_local), BF16),
            pltpu.VMEM((Q, 2, modes_local, NB * NB, k_local), F32),
            pltpu.VMEM((2 * NB * NB, k_local), F32),
            pltpu.VMEM((Q, 2 * NB * NB, k_local), F32),
        ],
        compiler_params=pltpu.CompilerParams(vmem_limit_bytes=56 << 20),
    )(coupling, re_rows, k_cols, near, everyone, owner, row)


def local(
    wannier_table,
    mode_matrix,
    re_coords,
    rp_coords,
    q_coords,
    k_coords,
    rotations,
    kq_owner,
    kq_row,
):
    e_local, r_local, _ = wannier_table.shape
    k_local = k_coords.shape[1]
    pairs = NB * NB
    cosine_q, sine_q = phases(q_coords, rp_coords)
    weights = jnp.stack(
        [jnp.stack([cosine_q, sine_q], axis=1), jnp.stack([-sine_q, cosine_q], axis=1)]
    )
    eye = jnp.eye(GROUP, dtype=BF16)
    phase = weights[:, :, :, None, None, :] * eye[None, None, None, :, :, None]
    phase = phase.reshape(2, Q * 2 * GROUP, GROUP * r_local)
    modes = jnp.repeat(mode_matrix.transpose(0, 2, 1).astype(BF16), pairs, axis=1)
    near = rotations.T
    everyone = lax.all_gather(near, "re", axis=0)
    partial = mix(phase, modes, wannier_table, lax.axis_size("rp"))
    owned = lax.psum_scatter(partial, "rp", scatter_dimension=0)
    coupling = lax.all_gather(owned, "re", axis=0)
    pad = ((0, 5), (0, 0))
    re_rows = jnp.pad(re_coords, pad).T.astype(BF16)
    k_cols = jnp.pad(k_coords, pad).astype(BF16)
    owner = kq_owner.reshape(Q, 1, k_local)
    row = kq_row.reshape(Q, 1, k_local)
    return bloch(coupling, re_rows, k_cols, near, everyone, owner, row)


def solution(mesh):
    in_specs = (
        P("re", "rp", None),
        P(),
        P(),
        P(None, "rp"),
        P(),
        P(None, "re"),
        P("re", None),
        P(None, "re", None),
        P(None, "re"),
    )
    out_specs = P(None, "rp", None, None, "re")
    return jax.shard_map(local, mesh=mesh, in_specs=in_specs, out_specs=out_specs, check_vma=False)
```

profile of v0, /device:TPU:0, one launch (start us, length us, event | category | flops | bytes accessed | tf_op | source)
XLA Modules:
  0.0 100.2 jit_solution(255085121533345277)
XLA Ops:
  7.4 0.0 reduce-scatter.2.cloned.1.call-start
  7.4 0.8 copy.28
  8.2 0.8 multiply_reduce_fusion
  9.0 0.1 cosine_convert_fusion
  9.1 0.1 fusion.4
  9.1 0.7 convert_bitcast_fusion
  9.8 0.1 copy.31
  9.9 0.1 mul.61
  10.0 0.1 mul.62
  10.2 0.1 mul.60
  10.4 0.1 broadcast_in_dim.2
  10.4 4.6 %copy-done = bf16[128,32,1536]{2,1,0:T(8,128)(2,1)S(1)} copy-done((bf16[128,32,1536]{2,1,0:T(8,128)(2,1)S(1)}, bf16[128,32,1536]{2,1,0:T(8,128)(2,1)}, u32[]{:S(2)}) %copy-start) | copy-done | bytes 12582936
  15.0 5.5 %shard_map.91 = bf16[4,2,192,256]{3,2,1,0:T(8,128)(2,1)} custom-call(bf16[2,32,256]{2,1,0:T(8,128)(2,1)S(1)} %broadcast_multiply_fusion.phase_ref, bf16[2,768,12]{2,1,0:T(8,128)(2,1)S(1)} %bitcast.23, bf16[128,32,1536]{2,1,0:T(8,128)(2,1)S(1)} %copy-done), custom_call_target="tpu_custom_call" | custom-call | tf_op jit(solution)/shard_map/pallas_call | solution.py:85
  20.5 0.0 all-gather.6.cloned.1.call-start
  20.6 0.8 copy.33
  21.3 0.0 all-gather.4.cloned.1.call-start
  21.4 25.2 %reduce-scatter.2.cloned.1.call-done = bf16[1,2,192,256]{3,2,1,0:T(8,128)(2,1)} async-done(((bf16[4,2,192,256]{3,2,1,0:T(8,128)(2,1)}), bf16[1,2,192,256]{3,2,1,0:T(8,128)(2,1)}) %reduce-scatter.2.cloned.1.call-update) | async-done | bytes 196624 | tf_op jit(solution)/shard_map/reduce_scatter | solution.py:250
  46.6 0.6 reshape.91.row_ref
  47.2 0.2 copy.32
  47.4 0.6 pad.11.k_ref
  48.0 0.8 pad_bitcast_fusion.re_ref
  48.8 0.1 all-gather.6.cloned.1.call-done
  48.9 27.2 %all-gather.4.cloned.1.call-done.coupling_ref = bf16[8,2,192,256]{3,2,1,0:T(8,128)(2,1)} async-done(((bf16[1,2,192,256]{3,2,1,0:T(8,128)(2,1)}), bf16[8,2,192,256]{3,2,1,0:T(8,128)(2,1)}) %all-gather.4.cloned.1.call-update) | async-done | bytes 1572880 | tf_op jit(solution)/shard_map/all_gather | solution.py:251
  76.1 16.7 %shard_map.92 = bf16[2,3,2,64,512]{4,3,2,1,0:T(8,128)(2,1)} custom-call(bf16[8,2,192,256]{3,2,1,0:T(8,128)(2,1)} %all-gather.4.cloned.1.call-done.coupling_ref, bf16[1024,8]{1,0:T(8,128)(2,1)} %pad_bitcast_fusion.re_ref, bf16[8,512]{1,0:T(8,128)(2,1)} %pad.11.k_ref, bf16[128,512]{1,0:T(8,128)(2,1)} %bitcast.25, bf16[8,128,512]{2,1,0:T(8,128)(2,1)} %bitcast.26, ...), custom_call_target="tpu_custom_call" | custom-call | tf_op jit(solution)/shard_map/pallas_call | solution.py:209
  (20 shorter events, 0.1 us)
Async XLA Ops:
  7.4 13.2 %copy-start.1 = (bf16[512,128]{1,0:T(8,128)(2,1)S(1)}, bf16[512,128]{1,0:T(8,128)(2,1)}, u32[]{:S(2)}) copy-start(bf16[512,128]{1,0:T(8,128)(2,1)} %param.15) | copy-start | bytes 393220
  7.4 39.2 %copy-start.3 = (s32[3,512]{1,0:T(4,128)S(1)}, s32[3,512]{1,0:T(4,128)}, u32[]{:S(2)}) copy-start(s32[3,512]{1,0:T(4,128)} %param.14) | copy-start | bytes 18436
  7.4 39.2 %copy-start.4 = (s32[2,512]{1,0:T(2,128)S(1)}, s32[2,512]{1,0:T(2,128)}, u32[]{:S(2)}) copy-start(s32[2,512]{1,0:T(2,128)} %param.17) | copy-start | bytes 12292
  7.4 39.8 %copy-start.2 = (s32[3,1024]{1,0:T(4,128)S(1)}, s32[3,1024]{1,0:T(4,128)}, u32[]{:S(2)}) copy-start(s32[3,1024]{1,0:T(4,128)} %param.11) | copy-start | bytes 36868
  7.4 39.2 %reduce-scatter.2.cloned.1.call-start = ((), (), s32[]{:S(2)}) async-start(), calls=%async_computation.1 | async-start | bytes 983040 | tf_op jit(solution)/shard_map/reduce_scatter | solution.py:250
  10.4 4.6 %copy-start = (bf16[128,32,1536]{2,1,0:T(8,128)(2,1)S(1)}, bf16[128,32,1536]{2,1,0:T(8,128)(2,1)}, u32[]{:S(2)}) copy-start(bf16[128,32,1536]{2,1,0:T(8,128)(2,1)} %table_ref.1) | copy-start | bytes 37748740
  20.5 28.4 %all-gather.6.cloned.1.call-start = ((), (), s32[]{:S(2)}) async-start(), calls=%async_computation.3 | async-start | bytes 1179648 | tf_op jit(solution)/shard_map/all_gather | solution.py:248
  21.3 54.8 %all-gather.4.cloned.1.call-start = ((), (), s32[]{:S(2)}) async-start(), calls=%async_computation.2 | async-start | bytes 1769472 | tf_op jit(solution)/shard_map/all_gather | solution.py:251
Sparse Core Ops, SparseCore 0:
  20.6 25.8 reduce-scatter.1
Sparse Core Ops, SparseCore 1:
  22.9 25.9 all-gather.5
  50.6 25.4 all-gather.3
where the time goes:
time: 101 us; the launch traced here: 100 us
  waiting for transfers between devices  52.5 us (52%)
  Pallas kernels  22.2 us (22%)
  between operations  15 us (15%)
  local copies, waits for them, and re-layouts  8.83 us (9%)
  other arithmetic  1.63 us (2%)
    all_gather x1, waiting for transfers between devices, local(): coupling = lax.all_gather(owned, 're', axis=0)  27.2 us
    reduce_scatter x1, waiting for transfers between devices, local(): owned = lax.psum_scatter(partial, 'rp', scatter_dimension=0)  25.2 us
    pallas_call x1, Pallas kernels, bloch(): pl.pallas_call(bloch_kernel, in_specs=[pl.BlockSpec(memory_space=pltpu.VM...  16.7 us
    unnamed x12, local copies, waits for them, and re-layouts  6.17 us
    pallas_call x1, Pallas kernels, mix(): pl.pallas_call(mix_kernel, grid=(e_local // block,), in_specs=[pl.BlockSp...  5.47 us
  transfers between devices with their start and end apart: 3, of which 3 were waited for; matrix products, arithmetic and copies ran while one was open for 3% of the time, Pallas kernels for 0%

commit v1 on v0

--- a/solution.py
+++ b/solution.py
@@ -96,8 +96,128 @@
             pltpu.VMEM((Q, 2 * e_local, width), BF16),
             pltpu.VMEM((Q, width, width), BF16),
         ],
-        compiler_params=pltpu.CompilerParams(vmem_limit_bytes=40 << 20),
+        compiler_params=pltpu.CompilerParams(vmem_limit_bytes=56 << 20),
     )(phase, modes, table)
+
+
+MESH = pl.DeviceIdType.MESH
+
+
+def send(source, target, send_sem, recv_sem, device):
+    return pltpu.make_async_remote_copy(
+        src_ref=source, dst_ref=target, send_sem=send_sem, recv_sem=recv_sem,
+        device_id=device, device_id_type=MESH,
+    )
+
+
+def exchange_kernel(
+    partial_ref, near_ref, coupling_ref, all_ref,
+    inbox, sum_send, sum_recv, far_send, far_recv, pair_send, pair_recv,
+):
+    shares, _, depth, _ = partial_ref.shape
+    half = coupling_ref.shape[0] // 2
+    me, row = lax.axis_index("re"), lax.axis_index("rp")
+    mate = me ^ 1
+    chunks = sum_send.shape[0]
+    rows = Q * depth // chunks
+
+    barrier = pltpu.get_barrier_semaphore()
+    peers = [(me, lax.rem(row + j, shares)) for j in range(1, shares)]
+    peers += [(me ^ (2 * j), row) for j in range(1, half)] + [(mate, row)]
+    for peer in peers:
+        pl.semaphore_signal(barrier, inc=1, device_id=peer, device_id_type=MESH)
+    pl.semaphore_wait(barrier, len(peers))
+
+    def piece(c):
+        q, first = divmod(c * rows, depth)
+        return q, pl.ds(first, rows)
+
+    waits = []
+    sums = {}
+    for c in range(chunks):
+        at = piece(c)
+        for j in range(1, shares):
+            to = lax.rem(row + j, shares)
+            copy = send(
+                partial_ref.at[(to,) + at], inbox.at[(j - 1,) + at],
+                sum_send.at[c, j - 1], sum_recv.at[c, j - 1], (me, to),
+            )
+            copy.start()
+            sums[c, j] = copy
+
+    def spread(c, block, whole):
+        own = []
+        for j in range(1, half):
+            copy = send(
+                block, whole(me), far_send.at[c, j], far_recv.at[c, j], (me ^ (2 * j), row)
+            )
+            copy.start()
+            own.append(copy)
+        copy = send(block, whole(me), pair_send.at[c, 0], pair_recv.at[c, 0], (mate, row))
+        copy.start()
+        waits.append(copy)
+        return own
+
+    def forward(c, own, whole):
+        for j in range(1, half):
+            own[j - 1].wait()
+            block = whole(me ^ (2 * j))
+            copy = send(block, block, pair_send.at[c, j], pair_recv.at[c, j], (mate, row))
+            copy.start()
+            waits.append(copy)
+
+    def rotations_of(d):
+        return all_ref.at[d]
+
+    def coupling_of(c):
+        at = piece(c)
+        return lambda d: coupling_ref.at[(d,) + at]
+
+    all_ref[me] = near_ref[...]
+    spreads = [spread(chunks, near_ref, rotations_of)]
+    wholes = [rotations_of]
+    order = [chunks]
+    for c in range(chunks):
+        at = piece(c)
+        total = partial_ref[(row,) + at].astype(F32)
+        for j in range(1, shares):
+            sums[c, j].wait()
+            total = total + inbox[(j - 1,) + at].astype(F32)
+        coupling_ref[(me,) + at] = total.astype(BF16)
+        spreads.append(spread(c, coupling_of(c)(me), coupling_of(c)))
+        wholes.append(coupling_of(c))
+        order.append(c)
+        forward(order[-2], spreads[-2], wholes[-2])
+    forward(order[-1], spreads[-1], wholes[-1])
+    for copy in waits:
+        copy.wait()
+
+
+def exchange(partial, near, devices):
+    shares, _, depth, twice = partial.shape
+    chunks = Q * 2
+    half = devices // 2
+    return pl.pallas_call(
+        exchange_kernel,
+        in_specs=[pl.BlockSpec(memory_space=pltpu.VMEM)] * 2,
+        out_specs=[pl.BlockSpec(memory_space=pltpu.VMEM)] * 2,
+        out_shape=[
+            jax.ShapeDtypeStruct((devices, Q, depth, twice), BF16),
+            jax.ShapeDtypeStruct((devices,) + near.shape, BF16),
+        ],
+        scratch_shapes=[
+            pltpu.VMEM((shares - 1, Q, depth, twice), BF16),
+            pltpu.SemaphoreType.DMA((chunks, shares - 1)),
+            pltpu.SemaphoreType.DMA((chunks, shares - 1)),
+            pltpu.SemaphoreType.DMA((chunks + 1, half)),
+            pltpu.SemaphoreType.DMA((chunks + 1, half)),
+            pltpu.SemaphoreType.DMA((chunks + 1, half)),
+            pltpu.SemaphoreType.DMA((chunks + 1, half)),
+        ],
+        compiler_params=pltpu.CompilerParams(
+            collective_id=0, has_side_effects=True, vmem_limit_bytes=16 << 20
+        ),
+    )(partial, near)
 
 
 def bloch_kernel(
@@ -218,7 +338,7 @@
             pltpu.VMEM((2 * NB * NB, k_local), F32),
             pltpu.VMEM((Q, 2 * NB * NB, k_local), F32),
         ],
-        compiler_params=pltpu.CompilerParams(vmem_limit_bytes=56 << 20),
+        compiler_params=pltpu.CompilerParams(vmem_limit_bytes=24 << 20),
     )(coupling, re_rows, k_cols, near, everyone, owner, row)
 
 
@@ -245,10 +365,8 @@
     phase = phase.reshape(2, Q * 2 * GROUP, GROUP * r_local)
     modes = jnp.repeat(mode_matrix.transpose(0, 2, 1).astype(BF16), pairs, axis=1)
     near = rotations.T
-    everyone = lax.all_gather(near, "re", axis=0)
     partial = mix(phase, modes, wannier_table, lax.axis_size("rp"))
-    owned = lax.psum_scatter(partial, "rp", scatter_dimension=0)
-    coupling = lax.all_gather(owned, "re", axis=0)
+    coupling, everyone = exchange(partial, near, lax.axis_size("re"))
     pad = ((0, 5), (0, 0))
     re_rows = jnp.pad(re_coords, pad).T.astype(BF16)
     k_cols = jnp.pad(k_coords, pad).astype(BF16)

time: 101 us -> 60.8 us (0.60)
  waiting for transfers between devices: 52.5 us -> 0 us
  Pallas kernels: 22.2 us -> 54.5 us
  between operations: 15 us -> 0.15 us
  local copies, waits for them, and re-layouts: 8.83 us -> 3.61 us
    pallas_call x0 -> x1, Pallas kernels: none -> 29.2 us  [exchange(): pl.pallas_call(exchange_kernel, in_specs=[pl.BlockSpec(memory_space=pltpu...]
    all_gather x2 -> x0, waiting for transfers between devices: 27.3 us -> none  [the longest x1 27.2 us: local(): coupling = lax.all_gather(owned, 're', axis=0)]
    reduce_scatter x1 -> x0, waiting for transfers between devices: 25.2 us -> none  [local(): owned = lax.psum_scatter(partial, 'rp', scatter_dimension=0)]
    pallas_call x1, Pallas kernels: 5.47 us -> 10.5 us  [mix(): pl.pallas_call(mix_kernel, grid=(e_local // block,), in_specs=[pl.BlockSp...]
    unnamed x12 -> x14, local copies, waits for them, and re-layouts: 6.17 us -> 2.06 us
    pallas_call x1, Pallas kernels: 16.7 us -> 14.8 us  [bloch(): pl.pallas_call(bloch_kernel, in_specs=[pl.BlockSpec(memory_space=pltpu.VM...]
  transfers between devices with their start and end apart: 3 -> 0, of which waited for: 3 -> 0; matrix products, arithmetic and copies ran while one was open for 3% -> 0% of each run, Pallas kernels for 0% -> 0%
where the time goes in v1:
time: 60.8 us; the launch traced here: 60.5 us
  Pallas kernels  54.5 us (90%)
  local copies, waits for them, and re-layouts  3.61 us (6%)
  other arithmetic  2.23 us (4%)
    pallas_call x1, Pallas kernels, exchange(): pl.pallas_call(exchange_kernel, in_specs=[pl.BlockSpec(memory_space=pltpu...  29.2 us
    pallas_call x1, Pallas kernels, bloch(): pl.pallas_call(bloch_kernel, in_specs=[pl.BlockSpec(memory_space=pltpu.VM...  14.8 us
    pallas_call x1, Pallas kernels, mix(): pl.pallas_call(mix_kernel, grid=(e_local // block,), in_specs=[pl.BlockSp...  10.5 us
    unnamed x14, local copies, waits for them, and re-layouts  2.06 us

profile of v1, /device:TPU:0, one launch (start us, length us, event | category | flops | bytes accessed | tf_op | source)
XLA Modules:
  0.0 60.5 jit_solution(10125734502233764563)
XLA Ops:
  0.0 0.8 %copy.22 = s32[3,2]{1,0:T(4,128)S(1)} copy(s32[3,2]{0,1:T(2,128)} %param.13) | data formatting | bytes 48 | tf_op args[4]
  0.8 0.8 %multiply_reduce_fusion = s32[2,32]{1,0:T(2,128)S(1)} fusion(s32[3,32]{1,0:T(4,128)} %param.12, s32[3,2]{1,0:T(4,128)S(1)} %copy.22), kind=kLoop, calls=%fused_computation.5 | loop fusion | flops 320 | bytes 664 | tf_op jit(solution)/shard_map/reduce_sum | solution.py:21
  1.6 0.1 fusion.4
  1.6 0.1 cosine_convert_fusion
  1.8 0.1 mul.60
  1.9 0.1 mul.61
  2.0 0.1 mul.62
  2.1 0.6 %broadcast_multiply_fusion.phase_ref = bf16[2,32,256]{2,1,0:T(8,128)(2,1)} fusion(bf16[2,32,256]{2,1,0:T(8,128)(2,1)S(1)} %mul.60, bf16[32,256]{1,0:T(8,128)(2,1)S(1)} %mul.62), kind=kLoop, calls=%fused_computation.1 | loop fusion | flops 16384 | bytes 81920 | tf_op jit(solution)/shard_map/mul | solution.py:364
  2.7 0.7 %convert_bitcast_fusion = bf16[2,12,12]{1,0,2:T(2,128)(2,1)S(1)} fusion(f32[2,12,12]{2,0,1:T(2,128)} %param.10), kind=kLoop, calls=%fused_computation.2 | loop fusion | flops 288 | bytes 1728 | tf_op jit(solution)/shard_map/convert_element_type | solution.py:366
  3.4 0.1 copy.25
  3.5 0.8 %broadcast_in_dim.2 = bf16[2,12,64,12]{3,2,1,0:T(8,128)(2,1)} broadcast(bf16[2,12,12]{2,1,0:T(8,128)(2,1)S(1)} %copy.25), dimensions={0,1,3} | broadcast | bytes 37440 | tf_op jit(solution)/shard_map/broadcast_in_dim | solution.py:366
  4.3 10.5 %shard_map.91.partial_ref = bf16[4,2,192,256]{3,2,1,0:T(8,128)(2,1)} custom-call(bf16[2,32,256]{2,1,0:T(8,128)(2,1)} %broadcast_multiply_fusion.phase_ref, bf16[2,768,12]{2,1,0:T(8,128)(2,1)} %bitcast.25, bf16[128,32,1536]{2,1,0:T(8,128)(2,1)} %table_ref.1), custom_call_target="tpu_custom_call" | custom-call | tf_op jit(solution)/shard_map/pallas_call | solution.py:85
  14.8 0.0 copy-done.2
  14.8 0.1 copy.26
  14.9 0.0 copy-start
  14.9 1.1 %copy-done = bf16[4,2,192,256]{3,2,1,0:T(8,128)(2,1)S(1)} copy-done((bf16[4,2,192,256]{3,2,1,0:T(8,128)(2,1)S(1)}, bf16[4,2,192,256]{3,2,1,0:T(8,128)(2,1)}, u32[]{:S(2)}) %copy-start) | copy-done | bytes 786456
  16.1 29.2 %shard_map.92 = (bf16[8,2,192,256]{3,2,1,0:T(8,128)(2,1)S(1)}, bf16[8,128,512]{2,1,0:T(8,128)(2,1)S(1)}) custom-call(bf16[4,2,192,256]{3,2,1,0:T(8,128)(2,1)S(1)} %copy-done, bf16[128,512]{1,0:T(8,128)(2,1)S(1)} %bitcast.22), custom_call_target="tpu_custom_call" | custom-call | tf_op jit(solution)/shard_map/pallas_call | solution.py:200
  45.3 0.0 copy-done.3
  45.3 0.2 copy.27
  45.6 0.1 pad_bitcast_fusion.re_ref
  45.6 0.0 copy-done.4
  45.7 0.0 copy-done.5
  45.7 0.0 copy-done.1
  45.7 14.8 %shard_map.93 = bf16[2,3,2,64,512]{4,3,2,1,0:T(8,128)(2,1)} custom-call(bf16[8,2,192,256]{3,2,1,0:T(8,128)(2,1)S(1)} %get-tuple-element.7.coupling_ref, bf16[1024,8]{1,0:T(8,128)(2,1)S(1)} %pad_bitcast_fusion.re_ref, bf16[8,512]{1,0:T(8,128)(2,1)S(1)} %pad.11.k_ref, bf16[128,512]{1,0:T(8,128)(2,1)S(1)} %bitcast.23, ...), custom_call_target="tpu_custom_call" | custom-call | tf_op jit(solution)/shard_map/pallas_call | solution.py:329
  (14 shorter events, 0.1 us)
Async XLA Ops:
  0.0 14.8 %copy-start.2 = (bf16[512,128]{1,0:T(8,128)(2,1)S(1)}, bf16[512,128]{1,0:T(8,128)(2,1)}, u32[]{:S(2)}) copy-start(bf16[512,128]{1,0:T(8,128)(2,1)} %param.15) | copy-start | bytes 393220
  0.0 45.3 %copy-start.3 = (s32[3,1024]{1,0:T(4,128)S(1)}, s32[3,1024]{1,0:T(4,128)}, u32[]{:S(2)}) copy-start(s32[3,1024]{1,0:T(4,128)} %param.11) | copy-start | bytes 36868
  0.0 45.6 %copy-start.4 = (s32[3,512]{1,0:T(4,128)S(1)}, s32[3,512]{1,0:T(4,128)}, u32[]{:S(2)}) copy-start(s32[3,512]{1,0:T(4,128)} %param.14) | copy-start | bytes 18436
  0.0 45.7 %copy-start.5 = (s32[2,512]{1,0:T(2,128)S(1)}, s32[2,512]{1,0:T(2,128)}, u32[]{:S(2)}) copy-start(s32[2,512]{1,0:T(2,128)} %param.17) | copy-start | bytes 12292
  0.0 45.7 %copy-start.1 = (s32[2,512,1]{1,2,0:T(1,128)S(1)}, s32[2,512,1]{1,2,0:T(1,128)}, u32[]{:S(2)}) copy-start(s32[2,512,1]{1,2,0:T(1,128)} %param.16) | copy-start | bytes 12292
  14.9 1.1 %copy-start = (bf16[4,2,192,256]{3,2,1,0:T(8,128)(2,1)S(1)}, bf16[4,2,192,256]{3,2,1,0:T(8,128)(2,1)}, u32[]{:S(2)}) copy-start(bf16[4,2,192,256]{3,2,1,0:T(8,128)(2,1)} %shard_map.91.partial_ref) | copy-start | bytes 2359300

commit v2 on v0

--- a/solution.py
+++ b/solution.py
@@ -96,32 +96,100 @@
             pltpu.VMEM((Q, 2 * e_local, width), BF16),
             pltpu.VMEM((Q, width, width), BF16),
         ],
-        compiler_params=pltpu.CompilerParams(vmem_limit_bytes=40 << 20),
+        compiler_params=pltpu.CompilerParams(vmem_limit_bytes=50 << 20),
     )(phase, modes, table)
 
 
+MESH = pl.DeviceIdType.MESH
+
+
+def send(source, target, send_sem, recv_sem, device):
+    return pltpu.make_async_remote_copy(
+        src_ref=source, dst_ref=target, send_sem=send_sem, recv_sem=recv_sem,
+        device_id=device, device_id_type=MESH,
+    )
+
+
 def bloch_kernel(
-    coupling_ref, re_ref, k_ref, near_ref, all_ref, owner_ref, row_ref, out_ref,
-    cosine, sine, summed, near, far,
+    partial_ref, near_ref, re_ref, k_ref, owner_ref, row_ref, out_ref,
+    coupling_ref, all_ref, inbox, cosine, sine, summed, near, far,
+    sum_send, sum_recv, far_send, far_recv, pair_send, pair_recv,
 ):
+    shares = partial_ref.shape[0]
     devices, _, depth, twice = coupling_ref.shape
+    half = devices // 2
     e_local = twice // 2
     k_local = k_ref.shape[1]
-    modes_local = depth // (NB * NB)
     pairs = NB * NB
+    modes_local = depth // pairs
+    chunks = Q * modes_local
+    me, place = lax.axis_index("re"), lax.axis_index("rp")
+    mate = me ^ 1
+
+    barrier = pltpu.get_barrier_semaphore()
+    peers = [(me, lax.rem(place + j, shares)) for j in range(1, shares)]
+    peers += [(me ^ (2 * j), place) for j in range(1, half)] + [(mate, place)]
+    for peer in peers:
+        pl.semaphore_signal(barrier, inc=1, device_id=peer, device_id_type=MESH)
+    pl.semaphore_wait(barrier, len(peers))
+
+    def piece(c):
+        q, v = divmod(c, modes_local)
+        return q, pl.ds(v * pairs, pairs)
+
+    sums = {}
+    for c in range(chunks):
+        at = piece(c)
+        for j in range(1, shares):
+            to = lax.rem(place + j, shares)
+            copy = send(
+                partial_ref.at[(to,) + at], inbox.at[(j - 1,) + at],
+                sum_send.at[c, j - 1], sum_recv.at[c, j - 1], (me, to),
+            )
+            copy.start()
+            sums[c, j] = copy
+
+    spreads, waits, wholes = {}, {}, {}
+
+    def spread(c, block, whole):
+        wholes[c] = whole
+        spreads[c] = []
+        copy = send(block, whole(me), pair_send.at[c, 0], pair_recv.at[c, 0], (mate, place))
+        for j in range(1, half):
+            far_copy = send(
+                block, whole(me), far_send.at[c, j], far_recv.at[c, j], (me ^ (2 * j), place)
+            )
+            far_copy.start()
+            spreads[c].append(far_copy)
+        copy.start()
+        waits[c] = [copy]
+
+    def forward(c):
+        for j in range(1, half):
+            spreads[c][j - 1].wait()
+            block = wholes[c](me ^ (2 * j))
+            copy = send(block, block, pair_send.at[c, j], pair_recv.at[c, j], (mate, place))
+            copy.start()
+            waits[c].append(copy)
+
+    def collect(c):
+        for copy in waits[c]:
+            copy.wait()
+
+    def add_up(c):
+        at = piece(c)
+        total = partial_ref[(place,) + at].astype(F32)
+        for j in range(1, shares):
+            sums[c, j].wait()
+            total = total + inbox[(j - 1,) + at].astype(F32)
+        coupling_ref[(me,) + at] = total.astype(BF16)
+        whole = lambda d: coupling_ref.at[(d,) + at]
+        spread(c, whole(me), whole)
+
+    all_ref[me] = near_ref[...]
+    spread(chunks, near_ref, lambda d: all_ref.at[d])
+
     near[...] = near_ref[...].astype(F32)
-
-    @pl.loop(0, Q)
-    def _(q):
-        rows = lax.broadcasted_iota(jnp.int32, (k_local, k_local), 0)
-        hot = (rows == row_ref[q]).astype(F32).astype(BF16)
-        owner = owner_ref[q]
-        far[q] = jnp.zeros(far.shape[1:], F32)
-
-        @pl.loop(0, devices)
-        def _(d):
-            found = jnp.dot(all_ref[d], hot, preferred_element_type=F32)
-            far[q] = jnp.where(owner == d, found, far[q])
 
     @pl.loop(0, devices)
     def _(d):
@@ -134,14 +202,30 @@
         folded = jnp.maximum(jnp.minimum(turns, 0.5 - turns), -0.5 - turns)
         sine[pl.ds(start, e_local), :] = sine_turn(folded).astype(BF16)
 
+    def look_up(q):
+        rows = lax.broadcasted_iota(jnp.int32, (k_local, k_local), 0)
+        hot = (rows == row_ref[q]).astype(F32).astype(BF16)
+        owner = owner_ref[q]
+        far[q] = jnp.zeros(far.shape[1:], F32)
+
+        @pl.loop(0, devices)
+        def _(d):
+            found = jnp.dot(all_ref[d], hot, preferred_element_type=F32)
+            far[q] = jnp.where(owner == d, found, far[q])
+
     tile = min(256, k_local)
-
-    @pl.loop(0, Q)
-    def _(q):
+    lanes = 128
+
+    def compute(c):
+        q, v = divmod(c, modes_local)
+        at = (q, pl.ds(v * pairs, pairs))
         left = jnp.concatenate(
             [
-                jnp.concatenate([coupling_ref[d, q, :, :e_local] for d in range(devices)], axis=1),
-                jnp.concatenate([coupling_ref[d, q, :, e_local:] for d in range(devices)], axis=1),
+                jnp.concatenate(
+                    [coupling_ref[(d,) + at][:, i * e_local : (i + 1) * e_local]
+                     for d in range(devices)], axis=1,
+                )
+                for i in range(2)
             ],
             axis=0,
         )
@@ -151,75 +235,97 @@
             cols = pl.ds(pl.multiple_of(j * tile, tile), tile)
             with_cos = jnp.dot(left, cosine[:, cols], preferred_element_type=F32)
             with_sin = jnp.dot(left, sine[:, cols], preferred_element_type=F32)
-            real = with_cos[:depth] - with_sin[depth:]
-            imag = with_cos[depth:] + with_sin[:depth]
-            for v in range(modes_local):
-                summed[q, 0, v, :, cols] = real[v * pairs : (v + 1) * pairs]
-                summed[q, 1, v, :, cols] = imag[v * pairs : (v + 1) * pairs]
-
-    lanes = 128
-    tiles = k_local // lanes
-
-    @pl.loop(0, Q * modes_local * tiles)
-    def _(i):
-        q = i // (modes_local * tiles)
-        v = (i // tiles) % modes_local
-        cols = pl.ds(pl.multiple_of((i % tiles) * lanes, lanes), lanes)
-
-        def spread(ref, lead, row):
-            return jnp.broadcast_to(ref[lead + (pl.ds(row, 1), cols)], (NB, lanes))
-
-        right_real = [near[pl.ds(b * NB, NB), cols] for b in range(NB)]
-        right_imag = [near[pl.ds(pairs + b * NB, NB), cols] for b in range(NB)]
-        half_real, half_imag = [], []
-        for a in range(NB):
-            real = imag = None
-            for b in range(NB):
-                c_real = spread(summed, (q, 0, v), a * NB + b)
-                c_imag = spread(summed, (q, 1, v), a * NB + b)
-                one = c_real * right_real[b] - c_imag * right_imag[b]
-                two = c_real * right_imag[b] + c_imag * right_real[b]
-                real = one if real is None else real + one
-                imag = two if imag is None else imag + two
-            half_real.append(real)
-            half_imag.append(imag)
-        for m in range(0, NB, 2):
-            reals, imags = [], []
-            for n in (m, m + 1):
+            summed[0, :, cols] = with_cos[:pairs] - with_sin[pairs:]
+            summed[1, :, cols] = with_cos[pairs:] + with_sin[:pairs]
+
+        @pl.loop(0, k_local // lanes)
+        def _(i):
+            cols = pl.ds(pl.multiple_of(i * lanes, lanes), lanes)
+
+            def fill(ref, lead, row):
+                return jnp.broadcast_to(ref[lead, pl.ds(row, 1), cols], (NB, lanes))
+
+            right_real = [near[pl.ds(b * NB, NB), cols] for b in range(NB)]
+            right_imag = [near[pl.ds(pairs + b * NB, NB), cols] for b in range(NB)]
+            half_real, half_imag = [], []
+            for a in range(NB):
                 real = imag = None
-                for a in range(NB):
-                    l_real = spread(far, (q,), a * NB + n)
-                    l_imag = spread(far, (q,), pairs + a * NB + n)
-                    one = l_real * half_real[a] + l_imag * half_imag[a]
-                    two = l_real * half_imag[a] - l_imag * half_real[a]
+                for b in range(NB):
+                    c_real = fill(summed, 0, a * NB + b)
+                    c_imag = fill(summed, 1, a * NB + b)
+                    one = c_real * right_real[b] - c_imag * right_imag[b]
+                    two = c_real * right_imag[b] + c_imag * right_real[b]
                     real = one if real is None else real + one
                     imag = two if imag is None else imag + two
-                reals.append(real)
-                imags.append(imag)
-            rows = pl.ds(m * NB, 2 * NB)
-            out_ref[q, v, 0, rows, cols] = jnp.concatenate(reals, axis=0).astype(BF16)
-            out_ref[q, v, 1, rows, cols] = jnp.concatenate(imags, axis=0).astype(BF16)
-
-
-def bloch(coupling, re_rows, k_cols, near, everyone, owner, row):
-    devices, _, depth, _ = coupling.shape
+                half_real.append(real)
+                half_imag.append(imag)
+            for m in range(0, NB, 2):
+                reals, imags = [], []
+                for n in (m, m + 1):
+                    real = imag = None
+                    for a in range(NB):
+                        l_real = fill(far, q, a * NB + n)
+                        l_imag = fill(far, q, pairs + a * NB + n)
+                        one = l_real * half_real[a] + l_imag * half_imag[a]
+                        two = l_real * half_imag[a] - l_imag * half_real[a]
+                        real = one if real is None else real + one
+                        imag = two if imag is None else imag + two
+                    reals.append(real)
+                    imags.append(imag)
+                rows = pl.ds(m * NB, 2 * NB)
+                out_ref[q, v, 0, rows, cols] = jnp.concatenate(reals, axis=0).astype(BF16)
+                out_ref[q, v, 1, rows, cols] = jnp.concatenate(imags, axis=0).astype(BF16)
+
+    lag = 3
+    for t in range(chunks + lag):
+        if t < chunks:
+            add_up(t)
+        if t == 0:
+            forward(chunks)
+        elif t <= chunks:
+            forward(t - 1)
+        if t == 1:
+            collect(chunks)
+        if 1 <= t <= Q:
+            look_up(t - 1)
+        if t >= lag:
+            collect(t - lag)
+            compute(t - lag)
+
+
+def bloch(partial, near, re_rows, k_cols, owner, row, devices):
+    shares, _, depth, twice = partial.shape
     e_all = re_rows.shape[0]
     k_local = k_cols.shape[1]
-    modes_local = depth // (NB * NB)
+    pairs = NB * NB
+    modes_local = depth // pairs
+    chunks = Q * modes_local
+    half = devices // 2
     return pl.pallas_call(
         bloch_kernel,
-        in_specs=[pl.BlockSpec(memory_space=pltpu.VMEM)] * 7,
+        in_specs=[pl.BlockSpec(memory_space=pltpu.VMEM)] * 6,
         out_specs=pl.BlockSpec(memory_space=pltpu.VMEM),
-        out_shape=jax.ShapeDtypeStruct((Q, modes_local, 2, NB * NB, k_local), BF16),
+        out_shape=jax.ShapeDtypeStruct((Q, modes_local, 2, pairs, k_local), BF16),
         scratch_shapes=[
+            pltpu.VMEM((devices, Q, depth, twice), BF16),
+            pltpu.VMEM((devices,) + near.shape, BF16),
+            pltpu.VMEM((shares - 1, Q, depth, twice), BF16),
             pltpu.VMEM((e_all, k_local), BF16),
             pltpu.VMEM((e_all, k_local), BF16),
-            pltpu.VMEM((Q, 2, modes_local, NB * NB, k_local), F32),
-            pltpu.VMEM((2 * NB * NB, k_local), F32),
-            pltpu.VMEM((Q, 2 * NB * NB, k_local), F32),
+            pltpu.VMEM((2, pairs, k_local), F32),
+            pltpu.VMEM((2 * pairs, k_local), F32),
+            pltpu.VMEM((Q, 2 * pairs, k_local), F32),
+            pltpu.SemaphoreType.DMA((chunks, shares - 1)),
+            pltpu.SemaphoreType.DMA((chunks, shares - 1)),
+            pltpu.SemaphoreType.DMA((chunks + 1, half)),
+            pltpu.SemaphoreType.DMA((chunks + 1, half)),
+            pltpu.SemaphoreType.DMA((chunks + 1, half)),
+            pltpu.SemaphoreType.DMA((chunks + 1, half)),
         ],
-        compiler_params=pltpu.CompilerParams(vmem_limit_bytes=56 << 20),
-    )(coupling, re_rows, k_cols, near, everyone, owner, row)
+        compiler_params=pltpu.CompilerParams(
+            collective_id=0, has_side_effects=True, vmem_limit_bytes=40 << 20
+        ),
+    )(partial, near, re_rows, k_cols, owner, row)
 
 
 def local(
@@ -245,16 +351,13 @@
     phase = phase.reshape(2, Q * 2 * GROUP, GROUP * r_local)
     modes = jnp.repeat(mode_matrix.transpose(0, 2, 1).astype(BF16), pairs, axis=1)
     near = rotations.T
-    everyone = lax.all_gather(near, "re", axis=0)
     partial = mix(phase, modes, wannier_table, lax.axis_size("rp"))
-    owned = lax.psum_scatter(partial, "rp", scatter_dimension=0)
-    coupling = lax.all_gather(owned, "re", axis=0)
     pad = ((0, 5), (0, 0))
     re_rows = jnp.pad(re_coords, pad).T.astype(BF16)
     k_cols = jnp.pad(k_coords, pad).astype(BF16)
     owner = kq_owner.reshape(Q, 1, k_local)
     row = kq_row.reshape(Q, 1, k_local)
-    return bloch(coupling, re_rows, k_cols, near, everyone, owner, row)
+    return bloch(partial, near, re_rows, k_cols, owner, row, lax.axis_size("re"))
 
 
 def solution(mesh):

time: 101 us -> 52.4 us (0.52)
  waiting for transfers between devices: 52.5 us -> 0 us
  Pallas kernels: 22.2 us -> 44.7 us
  between operations: 15 us -> 0.11 us
  local copies, waits for them, and re-layouts: 8.83 us -> 4.12 us
  other arithmetic: 1.63 us -> 3.05 us
    all_gather x2 -> x0, waiting for transfers between devices: 27.3 us -> none  [the longest x1 27.2 us: local(): coupling = lax.all_gather(owned, 're', axis=0)]
    reduce_scatter x1 -> x0, waiting for transfers between devices: 25.2 us -> none  [local(): owned = lax.psum_scatter(partial, 'rp', scatter_dimension=0)]
    pallas_call x1, Pallas kernels: 16.7 us -> 35.1 us  [bloch(): pl.pallas_call(bloch_kernel, in_specs=[pl.BlockSpec(memory_space=pltpu.VM...]
    pallas_call x1, Pallas kernels: 5.47 us -> 9.53 us  [mix(): pl.pallas_call(mix_kernel, grid=(e_local // block,), in_specs=[pl.BlockSp...]
    unnamed x12 -> x5, local copies, waits for them, and re-layouts: 6.17 us -> 2.67 us
    another operation x2, other arithmetic: 0.01 us -> 1.44 us
  transfers between devices with their start and end apart: 3 -> 0, of which waited for: 3 -> 0; matrix products, arithmetic and copies ran while one was open for 3% -> 0% of each run, Pallas kernels for 0% -> 0%
where the time goes in v2:
time: 52.4 us; the launch traced here: 51.9 us
  Pallas kernels  44.7 us (85%)
  local copies, waits for them, and re-layouts  4.12 us (8%)
  other arithmetic  3.05 us (6%)
    pallas_call x1, Pallas kernels, bloch(): pl.pallas_call(bloch_kernel, in_specs=[pl.BlockSpec(memory_space=pltpu.VM...  35.1 us
    pallas_call x1, Pallas kernels, mix(): pl.pallas_call(mix_kernel, grid=(e_local // block,), in_specs=[pl.BlockSp...  9.53 us
    unnamed x5, local copies, waits for them, and re-layouts  2.67 us
    another operation x2, other arithmetic  1.44 us

profile of v2, /device:TPU:0, one launch (start us, length us, event | category | flops | bytes accessed | tf_op | source)
XLA Modules:
  0.0 51.9 jit_solution(9342000013491624819)
XLA Ops:
  0.0 0.0 copy-start
  0.0 0.8 %copy.22 = s32[3,2]{1,0:T(4,128)S(1)} copy(s32[3,2]{0,1:T(2,128)} %param.13) | data formatting | bytes 48 | tf_op args[4]
  0.8 0.8 %multiply_reduce_fusion = s32[2,32]{1,0:T(2,128)S(1)} fusion(s32[3,32]{1,0:T(4,128)} %param.12, s32[3,2]{1,0:T(4,128)S(1)} %copy.22), kind=kLoop, calls=%fused_computation.5 | loop fusion | flops 320 | bytes 664 | tf_op jit(solution)/shard_map/reduce_sum | solution.py:21
  1.5 0.1 cosine_convert_fusion
  1.6 0.1 fusion.4
  1.7 0.7 %convert.9 = bf16[3,512]{1,0:T(4,128)(2,1)S(1)} convert(s32[3,512]{1,0:T(4,128)} %param.14) | non-fusion elementwise | flops 1536 | bytes 9216 | tf_op jit(solution)/shard_map/convert
  2.4 0.7 %reshape.91.row_ref = s32[2,1,512]{2,1,0:T(1,128)S(1)} reshape(s32[2,512]{1,0:T(2,128)} %param.17) | data formatting | bytes 8192 | tf_op jit(solution)/shard_map/reshape | solution.py:359
  3.1 0.7 %convert_bitcast_fusion = bf16[2,12,12]{1,0,2:T(2,128)(2,1)S(1)} fusion(f32[2,12,12]{2,0,1:T(2,128)} %param.10), kind=kLoop, calls=%fused_computation.2 | loop fusion | flops 288 | bytes 1728 | tf_op jit(solution)/shard_map/convert_element_type | solution.py:352
  3.8 0.1 copy.25
  3.9 0.7 %convert.8 = bf16[3,1024]{1,0:T(4,128)(2,1)S(1)} convert(s32[3,1024]{1,0:T(4,128)} %param.11) | non-fusion elementwise | flops 3072 | bytes 18432 | tf_op jit(solution)/shard_map/convert.2
  4.7 0.1 mul.61
  4.7 0.1 mul.62
  4.9 0.1 mul.60
  5.0 1.0 %copy.26 = bf16[512,128]{0,1:T(8,128)(2,1)S(1)} copy(bf16[512,128]{1,0:T(8,128)(2,1)} %param.15) | data formatting | bytes 262144 | tf_op args[6]
  6.0 0.2 copy.27
  6.2 0.1 pad_bitcast_fusion.re_ref
  6.3 0.1 broadcast_in_dim.2
  6.4 9.5 %shard_map.91.partial_ref = bf16[4,2,192,256]{3,2,1,0:T(8,128)(2,1)S(1)} custom-call(bf16[2,32,256]{2,1,0:T(8,128)(2,1)S(1)} %broadcast_multiply_fusion.phase_ref, bf16[2,768,12]{2,1,0:T(8,128)(2,1)S(1)} %bitcast.22, bf16[128,32,1536]{2,1,0:T(8,128)(2,1)} %table_ref.1), custom_call_target="tpu_custom_call" | custom-call | tf_op jit(solution)/shard_map/pallas_call | solution.py:85
  15.9 0.0 copy-done
  15.9 35.1 %shard_map.92 = bf16[2,3,2,64,512]{4,3,2,1,0:T(8,128)(2,1)S(1)} custom-call(bf16[4,2,192,256]{3,2,1,0:T(8,128)(2,1)S(1)} %shard_map.91.partial_ref, bf16[128,512]{1,0:T(8,128)(2,1)S(1)} %bitcast.23, bf16[1024,8]{1,0:T(8,128)(2,1)S(1)} %pad_bitcast_fusion.re_ref, bf16[8,512]{1,0:T(8,128)(2,1)S(1)} %pad.11.k_ref, s32[2,1,512]{2,1,0:T(1,128)S(1)} %bitcast.24, ...), custom_call_target="tpu_custom_call" | custom-call | tf_op jit(solution)/shard_map/pallas_call | solution.py:304
  51.1 0.9 %copy.31 = bf16[2,3,2,64,512]{4,3,2,1,0:T(8,128)(2,1)} copy(bf16[2,3,2,64,512]{4,3,2,1,0:T(8,128)(2,1)S(1)} %shard_map.92) | data formatting | bytes 1572864
  (7 shorter events, 0.1 us)
Async XLA Ops:
  0.0 15.9 %copy-start = (s32[2,512,1]{1,2,0:T(1,128)S(1)}, s32[2,512,1]{1,2,0:T(1,128)}, u32[]{:S(2)}) copy-start(s32[2,512,1]{1,2,0:T(1,128)} %param.16) | copy-start | bytes 12292

commit v3 on v2

--- a/solution.py
+++ b/solution.py
@@ -15,12 +15,6 @@
 GROUP = 8
 F32 = jnp.float32
 BF16 = jnp.bfloat16
-
-
-def phases(left, right):
-    products = jnp.sum(left[:, :, None] * right[:, None, :], axis=0)
-    angles = jnp.mod(products, GRID).astype(F32) * (2.0 * math.pi / GRID)
-    return (jnp.cos(angles).astype(BF16), jnp.sin(angles).astype(BF16))
 
 
 def sine_turn(turn):
@@ -33,7 +27,26 @@
     return x + x * (y * p)
 
 
-def mix_kernel(phase_ref, modes_ref, table_ref, out_ref, summed, kron):
+def cycle(turns):
+    turns = turns - jnp.floor(turns + 0.5)
+    folded = jnp.maximum(jnp.minimum(turns, 0.5 - turns), -0.5 - turns)
+    return sine_turn(0.25 - jnp.abs(turns)).astype(BF16), sine_turn(folded).astype(BF16)
+
+
+def narrow(integers):
+    return integers.astype(F32).astype(BF16)
+
+
+def inner(left, right):
+    return lax.dot_general(left, right, (((0,), (0,)), ((), ())), preferred_element_type=F32)
+
+
+def iota(shape, dim):
+    return lax.broadcasted_iota(jnp.int32, shape, dim)
+
+
+def mix_kernel(rp_ref, q_ref, modes_ref, table_ref, out_ref, summed, kron, phase):
+    pairs = NB * NB
     step = pl.program_id(0)
     block, r_local, both = table_ref.shape
     width = both // 2
@@ -42,23 +55,39 @@
 
     @pl.when(step == 0)
     def _():
-        shape = (MODES, width)
-        expand = (
-            lax.broadcasted_iota(jnp.int32, shape, 1) // (NB * NB)
-            == lax.broadcasted_iota(jnp.int32, shape, 0)
-        ).astype(F32).astype(BF16)
-        rows = lax.broadcasted_iota(jnp.int32, (width, width), 0) & (NB * NB - 1)
-        cols = lax.broadcasted_iota(jnp.int32, (width, width), 1) & (NB * NB - 1)
+        lanes_in = GROUP * r_local
+        tiling = (iota((r_local, lanes_in), 1) % r_local == iota((r_local, lanes_in), 0))
+        tiled = jnp.dot(narrow(rp_ref[...]), narrow(tiling), preferred_element_type=F32)
+        products = inner(narrow(q_ref[...]), tiled.astype(BF16))
+        shape = (Q * 2 * GROUP, lanes_in)
+        line = iota(shape, 0)
+        spread_out = jnp.broadcast_to(products[0:1], shape)
+        for q in range(1, Q):
+            spread_out = jnp.where(line // (2 * GROUP) == q, products[q : q + 1], spread_out)
+        cos_q, sin_q = cycle(spread_out * (1.0 / GRID))
+        cos_q, sin_q = cos_q.astype(F32), sin_q.astype(F32)
+        real = (line // GROUP) % 2 == 0
+        same = line % GROUP == iota(shape, 1) // r_local
+        phase[0] = jnp.where(same, jnp.where(real, cos_q, sin_q), 0.0).astype(BF16)
+        phase[1] = jnp.where(same, jnp.where(real, -sin_q, cos_q), 0.0).astype(BF16)
+
+        tall = narrow(iota((width, MODES), 0) // pairs == iota((width, MODES), 1))
+        wide = narrow(iota((MODES, width), 1) // pairs == iota((MODES, width), 0))
+        diagonal = iota((width, width), 0) % pairs == iota((width, width), 1) % pairs
         for q in range(Q):
-            spread = jnp.dot(modes_ref[q], expand, preferred_element_type=F32)
-            kron[q] = jnp.where(rows == cols, spread, 0.0).astype(BF16)
+            rows = lax.dot_general(
+                tall, modes_ref[q].astype(BF16), (((1,), (1,)), ((), ())),
+                preferred_element_type=F32,
+            )
+            full = jnp.dot(rows.astype(BF16), wide, preferred_element_type=F32)
+            kron[q] = jnp.where(diagonal, full, 0.0).astype(BF16)
 
     parts = []
     for g in range(block // GROUP):
         values = table_ref[g * GROUP : (g + 1) * GROUP].reshape(GROUP * r_local, both)
         parts.append(
-            jnp.dot(phase_ref[0], values[:, :width], preferred_element_type=F32)
-            + jnp.dot(phase_ref[1], values[:, width:], preferred_element_type=F32)
+            jnp.dot(phase[0], values[:, :width], preferred_element_type=F32)
+            + jnp.dot(phase[1], values[:, width:], preferred_element_type=F32)
         )
     for q in range(Q):
         for c in range(2):
@@ -77,7 +106,7 @@
                 out_ref[owner, q] = mixed[owner * depth : (owner + 1) * depth]
 
 
-def mix(phase, modes, table, owners):
+def mix(rp_coords, q_coords, modes, table, owners):
     e_local, r_local, both = table.shape
     width = both // 2
     block = 16
@@ -86,7 +115,8 @@
         mix_kernel,
         grid=(e_local // block,),
         in_specs=[
-            pl.BlockSpec(phase.shape, lambda i: (0, 0, 0)),
+            pl.BlockSpec(rp_coords.shape, lambda i: (0, 0)),
+            pl.BlockSpec(q_coords.shape, lambda i: (0, 0)),
             pl.BlockSpec(modes.shape, lambda i: (0, 0, 0)),
             pl.BlockSpec((block, r_local, both), lambda i: (i, 0, 0)),
         ],
@@ -95,9 +125,10 @@
         scratch_shapes=[
             pltpu.VMEM((Q, 2 * e_local, width), BF16),
             pltpu.VMEM((Q, width, width), BF16),
+            pltpu.VMEM((2, Q * 2 * GROUP, GROUP * r_local), BF16),
         ],
         compiler_params=pltpu.CompilerParams(vmem_limit_bytes=50 << 20),
-    )(phase, modes, table)
+    )(rp_coords, q_coords, modes, table)
 
 
 MESH = pl.DeviceIdType.MESH
@@ -186,26 +217,25 @@
         whole = lambda d: coupling_ref.at[(d,) + at]
         spread(c, whole(me), whole)
 
-    all_ref[me] = near_ref[...]
-    spread(chunks, near_ref, lambda d: all_ref.at[d])
-
-    near[...] = near_ref[...].astype(F32)
-
-    @pl.loop(0, devices)
+    near[...] = near_ref[...].astype(F32).T
+    all_ref[me] = near[...].astype(BF16)
+    spread(chunks, all_ref.at[me], lambda d: all_ref.at[d])
+
+    e_share = min(128, re_ref.shape[1])
+
+    @pl.loop(0, re_ref.shape[1] // e_share)
     def _(d):
-        start = pl.multiple_of(d * e_local, e_local)
-        turns = jnp.dot(
-            re_ref[pl.ds(start, e_local), :], k_ref[...], preferred_element_type=F32
-        ) * (1.0 / GRID)
-        turns = turns - jnp.floor(turns + 0.5)
-        cosine[pl.ds(start, e_local), :] = sine_turn(0.25 - jnp.abs(turns)).astype(BF16)
-        folded = jnp.maximum(jnp.minimum(turns, 0.5 - turns), -0.5 - turns)
-        sine[pl.ds(start, e_local), :] = sine_turn(folded).astype(BF16)
+        start = pl.multiple_of(d * e_share, e_share)
+        cos_k, sin_k = cycle(
+            inner(narrow(re_ref[:, pl.ds(start, e_share)]), narrow(k_ref[...])) * (1.0 / GRID)
+        )
+        cosine[pl.ds(start, e_share), :] = cos_k
+        sine[pl.ds(start, e_share), :] = sin_k
 
     def look_up(q):
         rows = lax.broadcasted_iota(jnp.int32, (k_local, k_local), 0)
-        hot = (rows == row_ref[q]).astype(F32).astype(BF16)
-        owner = owner_ref[q]
+        hot = (rows == row_ref[q : q + 1, :]).astype(F32).astype(BF16)
+        owner = owner_ref[q : q + 1, :]
         far[q] = jnp.zeros(far.shape[1:], F32)
 
         @pl.loop(0, devices)
@@ -295,7 +325,7 @@
 
 def bloch(partial, near, re_rows, k_cols, owner, row, devices):
     shares, _, depth, twice = partial.shape
-    e_all = re_rows.shape[0]
+    e_all = re_rows.shape[1]
     k_local = k_cols.shape[1]
     pairs = NB * NB
     modes_local = depth // pairs
@@ -308,7 +338,7 @@
         out_shape=jax.ShapeDtypeStruct((Q, modes_local, 2, pairs, k_local), BF16),
         scratch_shapes=[
             pltpu.VMEM((devices, Q, depth, twice), BF16),
-            pltpu.VMEM((devices,) + near.shape, BF16),
+            pltpu.VMEM((devices, 2 * pairs, k_local), BF16),
             pltpu.VMEM((shares - 1, Q, depth, twice), BF16),
             pltpu.VMEM((e_all, k_local), BF16),
             pltpu.VMEM((e_all, k_local), BF16),
@@ -339,25 +369,11 @@
     kq_owner,
     kq_row,
 ):
-    e_local, r_local, _ = wannier_table.shape
     k_local = k_coords.shape[1]
-    pairs = NB * NB
-    cosine_q, sine_q = phases(q_coords, rp_coords)
-    weights = jnp.stack(
-        [jnp.stack([cosine_q, sine_q], axis=1), jnp.stack([-sine_q, cosine_q], axis=1)]
-    )
-    eye = jnp.eye(GROUP, dtype=BF16)
-    phase = weights[:, :, :, None, None, :] * eye[None, None, None, :, :, None]
-    phase = phase.reshape(2, Q * 2 * GROUP, GROUP * r_local)
-    modes = jnp.repeat(mode_matrix.transpose(0, 2, 1).astype(BF16), pairs, axis=1)
-    near = rotations.T
-    partial = mix(phase, modes, wannier_table, lax.axis_size("rp"))
-    pad = ((0, 5), (0, 0))
-    re_rows = jnp.pad(re_coords, pad).T.astype(BF16)
-    k_cols = jnp.pad(k_coords, pad).astype(BF16)
-    owner = kq_owner.reshape(Q, 1, k_local)
-    row = kq_row.reshape(Q, 1, k_local)
-    return bloch(partial, near, re_rows, k_cols, owner, row, lax.axis_size("re"))
+    devices, shares = lax.axis_size("re"), lax.axis_size("rp")
+    partial = mix(rp_coords, q_coords, mode_matrix, wannier_table, shares)
+    owner = kq_owner.reshape(Q, k_local)
+    return bloch(partial, rotations, re_coords, k_coords, owner, kq_row, devices)
 
 
 def solution(mesh):

time: 52.4 us -> 49 us (0.935)
  other arithmetic: 3.05 us -> 0 us
    another operation x4 -> x0, other arithmetic: 1.46 us -> none
    unnamed x5 -> x14, local copies, waits for them, and re-layouts: 2.67 us -> 3.78 us
    convert_element_type x3 -> x0, other arithmetic: 0.77 us -> none  [the longest x1 0.71 us: local(): mode_matrix.transpose(0, 2, 1).astype(BF16)]
    reduce_sum x1 -> x0, other arithmetic: 0.76 us -> none  [phases(): products = jnp.sum(left[:, :, None] * right[:, None, :], axis=0)]
    reshape x1 -> x0, local copies, waits for them, and re-layouts: 0.69 us -> none  [local(): row = kq_row.reshape(Q, 1, k_local)]
where the time goes in v3:
time: 49 us; the launch traced here: 48.8 us
  Pallas kernels  44.9 us (92%)
  local copies, waits for them, and re-layouts  3.78 us (8%)
    pallas_call x1, Pallas kernels, bloch(): pl.pallas_call(bloch_kernel, in_specs=[pl.BlockSpec(memory_space=pltpu.VM...  35.1 us
    pallas_call x1, Pallas kernels, mix(): pl.pallas_call(mix_kernel, grid=(e_local // block,), in_specs=[pl.BlockSp...  9.79 us
    unnamed x14, local copies, waits for them, and re-layouts  3.78 us

profile of v3, /device:TPU:0, one launch (start us, length us, event | category | flops | bytes accessed | tf_op | source)
XLA Modules:
  0.0 48.8 jit_solution(11551716100590382280)
XLA Ops:
  0.0 0.0 copy-start.3
  0.0 0.0 copy-start
  0.0 0.0 copy-start.2
  0.0 0.0 copy-start.1
  0.0 0.8 %copy.10.q_ref = s32[3,2]{1,0:T(4,128)S(1)} copy(s32[3,2]{0,1:T(2,128)} %param.13) | data formatting | bytes 48 | tf_op args[4]
  0.8 0.7 %copy.14 = s32[2,512,1]{1,0,2:T(2,128)S(1)} copy(s32[2,512,1]{1,2,0:T(1,128)} %param.16) | data formatting | bytes 8192
  1.5 0.7 %copy.11.modes_ref = f32[2,12,12]{2,1,0:T(8,128)S(1)} copy(f32[2,12,12]{2,0,1:T(2,128)} %param.10) | data formatting | bytes 2304 | tf_op args[1]
  2.2 0.0 copy-start.4
  2.2 0.7 %copy-done.4 = s32[3,32]{1,0:T(4,128)S(1)} copy-done((s32[3,32]{1,0:T(4,128)S(1)}, s32[3,32]{1,0:T(4,128)}, u32[]{:S(2)}) %copy-start.4) | copy-done | bytes 408
  2.9 9.8 %shard_map.91.partial_ref = bf16[4,2,192,256]{3,2,1,0:T(8,128)(2,1)S(1)} custom-call(s32[3,32]{1,0:T(4,128)S(1)} %copy-done.4, s32[3,2]{1,0:T(4,128)S(1)} %copy.10.q_ref, f32[2,12,12]{2,1,0:T(8,128)S(1)} %copy.11.modes_ref, bf16[128,32,1536]{2,1,0:T(8,128)(2,1)} %table_ref.1), custom_call_target="tpu_custom_call" | custom-call | tf_op jit(solution)/shard_map/pallas_call | solution.py:114
  12.7 0.0 copy-done.3
  12.7 0.0 copy-done
  12.7 0.0 copy-done.2
  12.7 0.0 copy-done.1
  12.7 35.1 %shard_map.92 = bf16[2,3,2,64,512]{4,3,2,1,0:T(8,128)(2,1)S(1)} custom-call(bf16[4,2,192,256]{3,2,1,0:T(8,128)(2,1)S(1)} %shard_map.91.partial_ref, bf16[512,128]{1,0:T(8,128)(2,1)S(1)} %copy-done, s32[3,1024]{1,0:T(4,128)S(1)} %copy-done.1, s32[3,512]{1,0:T(4,128)S(1)} %copy-done.2, s32[2,512]{1,0:T(2,128)S(1)} %bitcast.3, s32[2,512]{1,0:T(2,128)S(1)} %copy-done.3), custom_call_target="tpu_custom_call" | custom-call | tf_op jit(solution)/shard_map/pallas_call | solution.py:334
  47.9 0.9 %copy.16 = bf16[2,3,2,64,512]{4,3,2,1,0:T(8,128)(2,1)} copy(bf16[2,3,2,64,512]{4,3,2,1,0:T(8,128)(2,1)S(1)} %shard_map.92) | data formatting | bytes 1572864
Async XLA Ops:
  0.0 12.7 %copy-start.3 = (s32[2,512]{1,0:T(2,128)S(1)}, s32[2,512]{1,0:T(2,128)}, u32[]{:S(2)}) copy-start(s32[2,512]{1,0:T(2,128)} %row_ref.1) | copy-start | bytes 12292
  0.0 12.7 %copy-start = (bf16[512,128]{1,0:T(8,128)(2,1)S(1)}, bf16[512,128]{1,0:T(8,128)(2,1)}, u32[]{:S(2)}) copy-start(bf16[512,128]{1,0:T(8,128)(2,1)} %near_ref.1) | copy-start | bytes 393220
  0.0 12.7 %copy-start.2 = (s32[3,512]{1,0:T(4,128)S(1)}, s32[3,512]{1,0:T(4,128)}, u32[]{:S(2)}) copy-start(s32[3,512]{1,0:T(4,128)} %k_ref.1) | copy-start | bytes 18436
  0.0 12.7 %copy-start.1 = (s32[3,1024]{1,0:T(4,128)S(1)}, s32[3,1024]{1,0:T(4,128)}, u32[]{:S(2)}) copy-start(s32[3,1024]{1,0:T(4,128)} %re_ref.1) | copy-start | bytes 36868
  2.2 0.7 %copy-start.4 = (s32[3,32]{1,0:T(4,128)S(1)}, s32[3,32]{1,0:T(4,128)}, u32[]{:S(2)}) copy-start(s32[3,32]{1,0:T(4,128)} %rp_ref.1) | copy-start | bytes 1156
